TPU v7x, 32 devices: a whole 2x2x4 slice. The times are simulated.
32 devices in a mesh: rows: 16 (over z, y, core), maze: 2 (over x).
Axes of the slice: x: 2, y: 2, z: 4, core: 2. Of those that a mesh axis runs over, the one named last changes fastest.
Arguments:
- maze_walls: int32 [2, 128, 256], P('maze', 'rows'), may hold values 0 or 1
- goal_cell: int32 [2, 2], P('maze'), may hold values from 0 to 127
- start_hidden: bfloat16 [2, 32, 128, 256], P('maze', None, 'rows'), may hold values from -0.8984375 to 0.8984375
- start_cell: float32 [2, 32, 128, 256], P('maze', None, 'rows'), may hold values from -4 to 4
- cotangent: bfloat16 [2, 3, 32, 128, 256], P('maze', None, None, 'rows'), may hold values from -6 to 6
- gate_weights: bfloat16 [73728], P(('rows', 'maze')), may hold values from -0.25 to 0.25
- embed_table: float32 [3, 32], replicated, may hold values from -4 to 4
Outputs:
- grad_weights: float32 [73728], P(('rows', 'maze'))
- grad_table: float32 [3, 32], replicated
- grad_hidden: float32 [2, 32, 128, 256], P('maze', None, 'rows')
- grad_cell: float32 [2, 32, 128, 256], P('maze', None, 'rows')
Inputs may be any that keep to these rules, and one draw needn't show every extreme that they name: `maze_walls`: 0 for open cells, 1 for walls. `goal_cell`: goal row and column inside the grid.
All inputs are finite; a program needn't handle non-finite values. No bound on the sum of `maze_walls` on one device may be relied on, other than what follows from the above.
Results may differ from a plain program's by a relative error of at most 0.0044.
Values may be sent and summed in bfloat16 or wider, within the bound.
A program may use at most 64 MiB of HBM per device.

v0:
```python
import math
import jax
import jax.numpy as jnp
from jax import lax
from jax.sharding import PartitionSpec as P

goal_reach = 64.0


def extended(cells, sides, width):
    for axis, dim in sides:
        count = lax.axis_size(axis)
        ends = count - 1
        head = lax.slice_in_dim(cells, 0, width, axis=dim)
        tail = lax.slice_in_dim(cells, cells.shape[dim] - width, cells.shape[dim], axis=dim)
        cells = jnp.concatenate(
            [
                lax.ppermute(tail, axis, [(i, (i + 1) % count) for i in range(ends)]),
                cells,
                lax.ppermute(head, axis, [((i + 1) % count, i) for i in range(ends)]),
            ],
            axis=dim,
        )
    return cells


def tap_offsets():
    return [(row_off, col_off) for row_off in (-1, 0, 1) for col_off in (-1, 0, 1)]


def gate_conv(padded, kernel, row_count, col_count):
    summed = None
    for tap_index, (row_off, col_off) in enumerate(tap_offsets()):
        window = padded[
            :, 1 + row_off : 1 + row_off + row_count, 1 + col_off : 1 + col_off + col_count
        ]
        tap_term = jnp.einsum(
            "gc,crq->grq", kernel[tap_index], window, preferred_element_type=jnp.float32
        )
        summed = tap_term if summed is None else summed + tap_term
    return summed


def weight_grads(gate_grad, padded, row_count, col_count):
    pieces = []
    for row_off, col_off in tap_offsets():
        window = padded[
            :, 1 + row_off : 1 + row_off + row_count, 1 + col_off : 1 + col_off + col_count
        ]
        pieces.append(
            jnp.einsum("grq,crq->gc", gate_grad, window, preferred_element_type=jnp.float32)
        )
    return jnp.stack(pieces)


def per_device(
    maze_walls, goal_cell, start_hidden, start_cell, cotangent, gate_weights, embed_table
):
    row_count = maze_walls.shape[1]
    col_count = maze_walls.shape[2]
    hidden_width = start_hidden.shape[1]
    input_width = embed_table.shape[1]
    channels = input_width + hidden_width
    step_count = cotangent.shape[1]
    gathered = lax.all_gather(gate_weights, ("rows", "maze"), axis=0, tiled=True)
    kernel = gathered.reshape(9, 4 * hidden_width, channels)
    first_row = lax.axis_index("rows") * row_count
    row_pos = first_row + lax.broadcasted_iota(jnp.int32, (row_count, col_count), 0)
    col_pos = lax.broadcasted_iota(jnp.int32, (row_count, col_count), 1)
    distance = (jnp.abs(row_pos - goal_cell[0, 0]) + jnp.abs(col_pos - goal_cell[0, 1])).astype(
        jnp.float32
    )
    goal_bump = jnp.exp(-distance / goal_reach)
    wall_mask = (maze_walls[0] == 1).astype(jnp.float32)
    inputs = (
        embed_table[0][:, None, None] * (1.0 - wall_mask)
        + embed_table[1][:, None, None] * wall_mask
        + embed_table[2][:, None, None] * goal_bump
    ).astype(jnp.bfloat16)
    input_ext = extended(inputs, (("rows", 1),), 1)
    hidden = start_hidden[0]
    cell_state = start_cell[0]
    stored = []
    for step_index in range(step_count):
        hidden_ext = extended(hidden, (("rows", 1),), 1)
        padded = jnp.pad(jnp.concatenate([input_ext, hidden_ext], axis=0), ((0, 0), (0, 0), (1, 1)))
        pre_gate = gate_conv(padded, kernel, row_count, col_count)
        in_gate = jax.nn.sigmoid(pre_gate[:hidden_width])
        forget_gate = jax.nn.sigmoid(pre_gate[hidden_width : 2 * hidden_width] + 1.0)
        out_gate = jax.nn.sigmoid(pre_gate[2 * hidden_width : 3 * hidden_width])
        cand_gate = jnp.tanh(pre_gate[3 * hidden_width :])
        new_cell = forget_gate * cell_state + in_gate * cand_gate
        squash = jnp.tanh(new_cell)
        stored.append((padded, cell_state, in_gate, forget_gate, out_gate, cand_gate, squash))
        hidden = (out_gate * squash).astype(jnp.bfloat16)
        cell_state = new_cell
    carry_hidden = jnp.zeros((hidden_width, row_count, col_count), jnp.float32)
    carry_cell = jnp.zeros((hidden_width, row_count, col_count), jnp.float32)
    kernel_acc = jnp.zeros((9, 4 * hidden_width, channels), jnp.float32)
    input_acc = jnp.zeros((input_width, row_count, col_count), jnp.float32)
    for step_index in reversed(range(step_count)):
        padded, prev_cell, in_gate, forget_gate, out_gate, cand_gate, squash = stored[step_index]
        hid_grad = cotangent[0, step_index].astype(jnp.float32) + carry_hidden
        cell_grad = carry_cell + hid_grad * out_gate * (1.0 - squash * squash)
        gate_grad = jnp.concatenate(
            [
                cell_grad * cand_gate * in_gate * (1.0 - in_gate),
                cell_grad * prev_cell * forget_gate * (1.0 - forget_gate),
                hid_grad * squash * out_gate * (1.0 - out_gate),
                cell_grad * in_gate * (1.0 - cand_gate * cand_gate),
            ],
            axis=0,
        ).astype(jnp.bfloat16)
        step_kernel = weight_grads(gate_grad, padded, row_count, col_count)
        kernel_acc = kernel_acc + step_kernel
        grad_ext = extended(gate_grad, (("rows", 1),), 1)
        grad_padded = jnp.pad(grad_ext, ((0, 0), (0, 0), (1, 1)))
        stack_grad = None
        for tap_index, (row_off, col_off) in enumerate(tap_offsets()):
            window = grad_padded[
                :, 1 - row_off : 1 - row_off + row_count, 1 - col_off : 1 - col_off + col_count
            ]
            tap_term = jnp.einsum(
                "gc,grq->crq", kernel[tap_index], window, preferred_element_type=jnp.float32
            )
            stack_grad = tap_term if stack_grad is None else stack_grad + tap_term
        input_acc = input_acc + stack_grad[:input_width]
        carry_hidden = stack_grad[input_width:]
        carry_cell = cell_grad * forget_gate
    scale = 1.0 / math.sqrt(
        lax.axis_size("maze") * lax.axis_size("rows") * row_count * col_count * step_count
    )
    grad_weights = (
        lax.psum_scatter(kernel_acc.reshape(-1), ("rows", "maze"), scatter_dimension=0, tiled=True)
        * scale
    )
    pieces = jnp.stack(
        [
            jnp.sum(input_acc * (1.0 - wall_mask), axis=(1, 2)),
            jnp.sum(input_acc * wall_mask, axis=(1, 2)),
            jnp.sum(input_acc * goal_bump, axis=(1, 2)),
        ]
    )
    grad_table = lax.psum(pieces, ("rows", "maze")) * scale
    return (grad_weights, grad_table, carry_hidden[None], carry_cell[None])


def solution(mesh):
    return jax.shard_map(
        per_device,
        mesh=mesh,
        in_specs=(
            P("maze", "rows", None),
            P("maze", None),
            P("maze", None, "rows", None),
            P("maze", None, "rows", None),
            P("maze", None, None, "rows", None),
            P(("rows", "maze")),
            P(),
        ),
        out_specs=(
            P(("rows", "maze")),
            P(),
            P("maze", None, "rows", None),
            P("maze", None, "rows", None),
        ),
        check_vma=False,
    )
```

profile of v0, /device:TPU:8, one launch (start us, length us, event | category | flops | bytes accessed | tf_op | source)
XLA Modules:
  0.0 296.0 jit_solution(9705465087397272263)
XLA Ops:
  7.2 1.3 fusion.286
  9.2 0.8 slice_bitcast_fusion.3
  11.6 1.9 collective-permute-start
  13.5 4.5 %collective-permute-start.1 = (bf16[32,1,256]{2,0,1:T(8,128)(2,1)S(1)}, bf16[32,1,256]{2,0,1:T(8,128)(2,1)S(1)}, u32[]{:S(2)}, u32[]{:S(2)}) collective-permute-start(bf16[32,1,256]{2,0,1:T(8,128)(2,1)S(1)} %get-tuple-element.67), channel_id=1, source_target_pairs={{2,0},{4,2},{6,4},{8,6},{10,8},{12,10},{14,12},{16,14},{18,16},{20... | collective-permute-start | bytes 49160 | tf_op jit(solution)/shard_map/ppermute | solution.py:20
  18.1 0.9 copy.275
  19.0 1.9 collective-permute-start.2
  20.9 4.5 %collective-permute-start.3 = (bf16[32,1,256]{2,0,1:T(8,128)(2,1)S(1)}, bf16[32,1,256]{2,0,1:T(8,128)(2,1)S(1)}, u32[]{:S(2)}, u32[]{:S(2)}) collective-permute-start(bf16[32,1,256]{2,0,1:T(8,128)(2,1)S(1)} %get-tuple-element.69), channel_id=1, source_target_pairs={{2,0},{4,2},{6,4},{8,6},{10,8},{12,10},{14,12},{16,14},{18,16},{20... | collective-permute-start | bytes 49160 | tf_op jit(solution)/shard_map/ppermute | solution.py:20
  26.2 53.3 %all-gather = bf16[32,1,2304]{2,1,0:T(2,128)(2,1)S(1)} all-gather(bf16[1,1,2304]{2,1,0:T(2,128)(2,1)S(1)} %reshape.144), channel_id=1, replica_groups=mesh['rows'=16,'maze'=2] {'rows','maze'}, dimensions={0}, use_global_device_ids=true | all-gather | bytes 152064 | tf_op jit(solution)/shard_map/all_gather | solution.py:65
  79.5 0.8 reduce
  85.4 1.9 collective-permute-start.4
  87.4 6.4 %collective-permute-start.5 = (bf16[32,1,256]{2,0,1:T(8,128)(2,1)S(1)}, bf16[32,1,256]{2,0,1:T(8,128)(2,1)S(1)}, u32[]{:S(2)}, u32[]{:S(2)}) collective-permute-start(bf16[32,1,256]{2,0,1:T(8,128)(2,1)S(1)} %get-tuple-element.65), channel_id=1, source_target_pairs={{2,0},{4,2},{6,4},{8,6},{10,8},{12,10},{14,12},{16,14},{18,16},{20... | collective-permute-start | bytes 49160 | tf_op jit(solution)/shard_map/ppermute | solution.py:20
  93.8 1.4 collective-permute-done.5
  98.3 0.9 multiply_convert_fusion.10
  99.2 1.3 fusion.282
  100.6 1.9 collective-permute-start.6
  102.5 4.7 %collective-permute-start.7 = (bf16[32,1,256]{2,0,1:T(8,128)(2,1)}, bf16[32,1,256]{2,0,1:T(8,128)(2,1)}, u32[]{:S(2)}, u32[]{:S(2)}) collective-permute-start(bf16[32,1,256]{2,0,1:T(8,128)(2,1)} %get-tuple-element.63), channel_id=1, source_target_pairs={{2,0},{4,2},{6,4},{8,6},{10,8},{12,10},{14,12},{16,14},{18,16},{20... | collective-permute-start | bytes 49160 | tf_op jit(solution)/shard_map/ppermute | solution.py:20
  108.0 0.9 collective-permute-done.7
  108.8 0.9 maximum_maximum_fusion.2
  109.8 1.1 fusion.180
  116.3 1.9 collective-permute-start.8
  118.3 6.7 %collective-permute-start.9 = (bf16[128,1,256]{2,0,1:T(8,128)(2,1)S(1)}, bf16[128,1,256]{2,0,1:T(8,128)(2,1)S(1)}, u32[]{:S(2)}, u32[]{:S(2)}) collective-permute-start(bf16[128,1,256]{2,0,1:T(8,128)(2,1)S(1)} %get-tuple-element.49), channel_id=1, source_target_pairs={{2,0},{4,2},{6,4},{8,6},{10,8},{12,10},{14,12},{16,14},{18,16},{20... | collective-permute-start | bytes 196616 | tf_op jit(solution)/shard_map/ppermute | solution.py:20
  133.2 1.9 collective-permute-start.10
  135.1 4.6 %collective-permute-start.11 = (bf16[128,1,256]{2,0,1:T(8,128)(2,1)S(1)}, bf16[128,1,256]{2,0,1:T(8,128)(2,1)S(1)}, u32[]{:S(2)}, u32[]{:S(2)}) collective-permute-start(bf16[128,1,256]{2,0,1:T(8,128)(2,1)S(1)} %get-tuple-element.47), channel_id=1, source_target_pairs={{2,0},{4,2},{6,4},{8,6},{10,8},{12,10},{14,12},{16,14},{18,16},{20... | collective-permute-start | bytes 196616 | tf_op jit(solution)/shard_map/ppermute | solution.py:20
  148.1 1.9 collective-permute-start.12
  150.0 4.8 %collective-permute-start.13 = (bf16[128,1,256]{2,0,1:T(8,128)(2,1)S(1)}, bf16[128,1,256]{2,0,1:T(8,128)(2,1)S(1)}, u32[]{:S(2)}, u32[]{:S(2)}) collective-permute-start(bf16[128,1,256]{2,0,1:T(8,128)(2,1)S(1)} %get-tuple-element.45), channel_id=1, source_target_pairs={{2,0},{4,2},{6,4},{8,6},{10,8},{12,10},{14,12},{16,14},{18,16},{20... | collective-permute-start | bytes 196616 | tf_op jit(solution)/shard_map/ppermute | solution.py:20
  157.5 0.9 copy.141
  158.6 0.9 add.362
  163.0 0.7 copy-done.16
  164.8 0.9 copy.140
  165.7 39.5 %psum.7 = f32[3,32]{1,0:T(4,128)S(1)} all-reduce(f32[3,32]{1,0:T(4,128)S(1)} %pad_maximum_fusion.10), channel_id=1, replica_groups=mesh['rows'=16,'maze'=2] {'rows','maze'}, use_global_device_ids=true, to_apply=%region_4.5 | all-reduce | flops 96 | bytes 768 | tf_op jit(solution)/shard_map/psum | solution.py:144
  205.8 81.9 %all-reduce.9.cloned.1.call-done = f32[73728]{0:T(1024)} async-done(((f32[73728]{0:T(1024)}), f32[73728]{0:T(1024)}) %all-reduce.9.cloned.1.call-update) | async-done | bytes 294928
  287.7 1.4 dynamic-slice_multiply_fusion
  (194 shorter events, 41.4 us)
Async XLA Ops:
  7.2 280.6 %all-reduce.9.cloned.1.call-start = ((), (), s32[]{:S(2)}) async-start(), calls=%async_computation | async-start | bytes 589824
  10.7 14.8 %copy-start.25 = (f32[8,256]{1,0:T(8,128)}, f32[8,256]{1,0:T(8,128)S(1)}, u32[]{:S(2)}) copy-start(f32[8,256]{1,0:T(8,128)S(1)} %get-tuple-element.30) | copy-start | bytes 24580
  10.7 14.8 %copy-start.23 = (f32[8,256]{1,0:T(8,128)}, f32[8,256]{1,0:T(8,128)S(1)}, u32[]{:S(2)}) copy-start(f32[8,256]{1,0:T(8,128)S(1)} %convert_bitcast_fusion) | copy-start | bytes 24580
  11.4 14.1 %copy-start.27 = (f32[8,256]{1,0:T(8,128)}, f32[8,256]{1,0:T(8,128)S(1)}, u32[]{:S(2)}) copy-start(f32[8,256]{1,0:T(8,128)S(1)} %multiply_exponential_fusion) | copy-start | bytes 24580
  11.6 69.8 %collective-permute-start = (bf16[32,1,256]{2,0,1:T(8,128)(2,1)S(1)}, bf16[32,1,256]{2,0,1:T(8,128)(2,1)S(1)}, u32[]{:S(2)}, u32[]{:S(2)}) collective-permute-start(bf16[32,1,256]{2,0,1:T(8,128)(2,1)S(1)} %get-tuple-element.66), channel_id=1, source_target_pairs={{0,2},{2,4},{4,6},{6,8},{8,10},{10,12},{12,14},{14,16},{16,18},{18... | collective-permute-start | bytes 49160 | tf_op jit(solution)/shard_map/ppermute | solution.py:18
  13.5 67.9 %collective-permute-start.1 = (bf16[32,1,256]{2,0,1:T(8,128)(2,1)S(1)}, bf16[32,1,256]{2,0,1:T(8,128)(2,1)S(1)}, u32[]{:S(2)}, u32[]{:S(2)}) collective-permute-start(bf16[32,1,256]{2,0,1:T(8,128)(2,1)S(1)} %get-tuple-element.67), channel_id=1, source_target_pairs={{2,0},{4,2},{6,4},{8,6},{10,8},{12,10},{14,12},{16,14},{18,16},{20... | collective-permute-start | bytes 49160 | tf_op jit(solution)/shard_map/ppermute | solution.py:20
  19.0 62.4 %collective-permute-start.2 = (bf16[32,1,256]{2,0,1:T(8,128)(2,1)S(1)}, bf16[32,1,256]{2,0,1:T(8,128)(2,1)S(1)}, u32[]{:S(2)}, u32[]{:S(2)}) collective-permute-start(bf16[32,1,256]{2,0,1:T(8,128)(2,1)S(1)} %get-tuple-element.68), channel_id=1, source_target_pairs={{0,2},{2,4},{4,6},{6,8},{8,10},{10,12},{12,14},{14,16},{16,18},{18... | collective-permute-start | bytes 49160 | tf_op jit(solution)/shard_map/ppermute | solution.py:18
  20.9 60.5 %collective-permute-start.3 = (bf16[32,1,256]{2,0,1:T(8,128)(2,1)S(1)}, bf16[32,1,256]{2,0,1:T(8,128)(2,1)S(1)}, u32[]{:S(2)}, u32[]{:S(2)}) collective-permute-start(bf16[32,1,256]{2,0,1:T(8,128)(2,1)S(1)} %get-tuple-element.69), channel_id=1, source_target_pairs={{2,0},{4,2},{6,4},{8,6},{10,8},{12,10},{14,12},{16,14},{18,16},{20... | collective-permute-start | bytes 49160 | tf_op jit(solution)/shard_map/ppermute | solution.py:20
  80.8 16.8 %copy-start.7 = (bf16[128,64]{1,0:T(8,128)(2,1)}, bf16[128,64]{1,0:T(8,128)(2,1)S(1)}, u32[]{:S(2)}) copy-start(bf16[128,64]{1,0:T(8,128)(2,1)S(1)} %slice.531) | copy-start | bytes 49156
  81.0 15.6 %copy-start.9 = (bf16[128,64]{1,0:T(8,128)(2,1)}, bf16[128,64]{1,0:T(8,128)(2,1)S(1)}, u32[]{:S(2)}) copy-start(bf16[128,64]{1,0:T(8,128)(2,1)S(1)} %slice.522) | copy-start | bytes 49156
  81.2 14.7 %copy-start = (bf16[128,64]{1,0:T(8,128)(2,1)}, bf16[128,64]{1,0:T(8,128)(2,1)S(1)}, u32[]{:S(2)}) copy-start(bf16[128,64]{1,0:T(8,128)(2,1)S(1)} %slice.516) | copy-start | bytes 49156
  81.4 13.8 %copy-start.2 = (bf16[128,64]{1,0:T(8,128)(2,1)}, bf16[128,64]{1,0:T(8,128)(2,1)S(1)}, u32[]{:S(2)}) copy-start(bf16[128,64]{1,0:T(8,128)(2,1)S(1)} %slice.510) | copy-start | bytes 49156
  81.4 13.8 %copy-start.22 = (bf16[32,1,256]{2,0,1:T(8,128)(2,1)}, bf16[32,1,256]{2,0,1:T(8,128)(2,1)S(1)}, u32[]{:S(2)}) copy-start(bf16[32,1,256]{2,0,1:T(8,128)(2,1)S(1)} %collective-permute-done.1) | copy-start | bytes 49156
  84.2 1.0 copy-start.5
  85.4 10.1 %copy-start.12 = (bf16[128,64]{1,0:T(8,128)(2,1)S(1)}, bf16[128,64]{1,0:T(8,128)(2,1)}, u32[]{:S(2)}) copy-start(bf16[128,64]{1,0:T(8,128)(2,1)} %copy-done.11) | copy-start | bytes 49156
  85.4 8.3 %collective-permute-start.4 = (bf16[32,1,256]{2,0,1:T(8,128)(2,1)S(1)}, bf16[32,1,256]{2,0,1:T(8,128)(2,1)S(1)}, u32[]{:S(2)}, u32[]{:S(2)}) collective-permute-start(bf16[32,1,256]{2,0,1:T(8,128)(2,1)S(1)} %get-tuple-element.64), channel_id=1, source_target_pairs={{0,2},{2,4},{4,6},{6,8},{8,10},{10,12},{12,14},{14,16},{16,18},{18... | collective-permute-start | bytes 49160 | tf_op jit(solution)/shard_map/ppermute | solution.py:18
  87.4 7.8 %collective-permute-start.5 = (bf16[32,1,256]{2,0,1:T(8,128)(2,1)S(1)}, bf16[32,1,256]{2,0,1:T(8,128)(2,1)S(1)}, u32[]{:S(2)}, u32[]{:S(2)}) collective-permute-start(bf16[32,1,256]{2,0,1:T(8,128)(2,1)S(1)} %get-tuple-element.65), channel_id=1, source_target_pairs={{2,0},{4,2},{6,4},{8,6},{10,8},{12,10},{14,12},{16,14},{18,16},{20... | collective-permute-start | bytes 49160 | tf_op jit(solution)/shard_map/ppermute | solution.py:20
  98.3 9.0 %copy-start.21 = (bf16[1,3,32,8,256]{4,3,2,1,0:T(8,128)(2,1)S(1)}, bf16[1,3,32,8,256]{4,3,2,1,0:T(8,128)(2,1)}, u32[]{:S(2)}) copy-start(bf16[1,3,32,8,256]{4,3,2,1,0:T(8,128)(2,1)} %param.11) | copy-start | bytes 1179652
  100.6 7.4 %collective-permute-start.6 = (bf16[32,1,256]{2,0,1:T(8,128)(2,1)}, bf16[32,1,256]{2,0,1:T(8,128)(2,1)}, u32[]{:S(2)}, u32[]{:S(2)}) collective-permute-start(bf16[32,1,256]{2,0,1:T(8,128)(2,1)} %get-tuple-element.62), channel_id=1, source_target_pairs={{0,2},{2,4},{4,6},{6,8},{8,10},{10,12},{12,14},{14,16},{16,18},{18... | collective-permute-start | bytes 49160 | tf_op jit(solution)/shard_map/ppermute | solution.py:18
  102.5 6.4 %collective-permute-start.7 = (bf16[32,1,256]{2,0,1:T(8,128)(2,1)}, bf16[32,1,256]{2,0,1:T(8,128)(2,1)}, u32[]{:S(2)}, u32[]{:S(2)}) collective-permute-start(bf16[32,1,256]{2,0,1:T(8,128)(2,1)} %get-tuple-element.63), channel_id=1, source_target_pairs={{2,0},{4,2},{6,4},{8,6},{10,8},{12,10},{14,12},{16,14},{18,16},{20... | collective-permute-start | bytes 49160 | tf_op jit(solution)/shard_map/ppermute | solution.py:20
  108.0 2.9 copy-start.13
  116.3 11.3 %collective-permute-start.8 = (bf16[128,1,256]{2,0,1:T(8,128)(2,1)S(1)}, bf16[128,1,256]{2,0,1:T(8,128)(2,1)S(1)}, u32[]{:S(2)}, u32[]{:S(2)}) collective-permute-start(bf16[128,1,256]{2,0,1:T(8,128)(2,1)S(1)} %get-tuple-element.48), channel_id=1, source_target_pairs={{0,2},{2,4},{4,6},{6,8},{8,10},{10,12},{12,14},{14,16},{16,18},{18... | collective-permute-start | bytes 196616 | tf_op jit(solution)/shard_map/ppermute | solution.py:18
  118.3 9.4 %collective-permute-start.9 = (bf16[128,1,256]{2,0,1:T(8,128)(2,1)S(1)}, bf16[128,1,256]{2,0,1:T(8,128)(2,1)S(1)}, u32[]{:S(2)}, u32[]{:S(2)}) collective-permute-start(bf16[128,1,256]{2,0,1:T(8,128)(2,1)S(1)} %get-tuple-element.49), channel_id=1, source_target_pairs={{2,0},{4,2},{6,4},{8,6},{10,8},{12,10},{14,12},{16,14},{18,16},{20... | collective-permute-start | bytes 196616 | tf_op jit(solution)/shard_map/ppermute | solution.py:20
  131.4 0.9 copy-start.20
  131.6 0.9 copy-start.15
  133.2 9.2 %collective-permute-start.10 = (bf16[128,1,256]{2,0,1:T(8,128)(2,1)S(1)}, bf16[128,1,256]{2,0,1:T(8,128)(2,1)S(1)}, u32[]{:S(2)}, u32[]{:S(2)}) collective-permute-start(bf16[128,1,256]{2,0,1:T(8,128)(2,1)S(1)} %get-tuple-element.46), channel_id=1, source_target_pairs={{0,2},{2,4},{4,6},{6,8},{8,10},{10,12},{12,14},{14,16},{16,18},{18... | collective-permute-start | bytes 196616 | tf_op jit(solution)/shard_map/ppermute | solution.py:18
  135.1 7.3 %collective-permute-start.11 = (bf16[128,1,256]{2,0,1:T(8,128)(2,1)S(1)}, bf16[128,1,256]{2,0,1:T(8,128)(2,1)S(1)}, u32[]{:S(2)}, u32[]{:S(2)}) collective-permute-start(bf16[128,1,256]{2,0,1:T(8,128)(2,1)S(1)} %get-tuple-element.47), channel_id=1, source_target_pairs={{2,0},{4,2},{6,4},{8,6},{10,8},{12,10},{14,12},{16,14},{18,16},{20... | collective-permute-start | bytes 196616 | tf_op jit(solution)/shard_map/ppermute | solution.py:20
  146.5 0.9 copy-start.6
  148.1 11.4 %collective-permute-start.12 = (bf16[128,1,256]{2,0,1:T(8,128)(2,1)S(1)}, bf16[128,1,256]{2,0,1:T(8,128)(2,1)S(1)}, u32[]{:S(2)}, u32[]{:S(2)}) collective-permute-start(bf16[128,1,256]{2,0,1:T(8,128)(2,1)S(1)} %get-tuple-element.44), channel_id=1, source_target_pairs={{0,2},{2,4},{4,6},{6,8},{8,10},{10,12},{12,14},{14,16},{16,18},{18... | collective-permute-start | bytes 196616 | tf_op jit(solution)/shard_map/ppermute | solution.py:18
  150.0 9.5 %collective-permute-start.13 = (bf16[128,1,256]{2,0,1:T(8,128)(2,1)S(1)}, bf16[128,1,256]{2,0,1:T(8,128)(2,1)S(1)}, u32[]{:S(2)}, u32[]{:S(2)}) collective-permute-start(bf16[128,1,256]{2,0,1:T(8,128)(2,1)S(1)} %get-tuple-element.45), channel_id=1, source_target_pairs={{2,0},{4,2},{6,4},{8,6},{10,8},{12,10},{14,12},{16,14},{18,16},{20... | collective-permute-start | bytes 196616 | tf_op jit(solution)/shard_map/ppermute | solution.py:20
  162.7 1.0 copy-start.16
  162.7 1.2 copy-start.18
  (12 other events, 9.4 us)
Sparse Core Ops, SparseCore 0:
  159.6 128.1 all-reduce.8
where the time goes:
time: 297 us; the launch traced here: 296 us
  blocking collectives  92.8 us (31%)
  waiting for transfers between devices  84.2 us (28%)
  starting transfers between devices  49.7 us (17%)
  matrix products  27.1 us (9%)
  local copies, waits for them, and re-layouts  16 us (5%)
  between operations  15 us (5%)
  other arithmetic  11 us (4%)
    unnamed x2, waiting for transfers between devices  81.9 us
    all_gather x1, blocking collectives, per_device(): lax.all_gather(gate_weights, ('rows', 'maze'), axis=0, tiled=True)  53.3 us
    psum x1, blocking collectives, per_device(): grad_table = lax.psum(pieces, ('rows', 'maze')) * scale  39.5 us
    ppermute x7, starting transfers between devices, extended(): lax.ppermute(head, axis, [((i + 1) % count, i) for i in range(ends)])  36.2 us
    ppermute x7, starting transfers between devices, extended(): lax.ppermute(tail, axis, [(i, (i + 1) % count) for i in range(ends)])  13.4 us
    unnamed x63, local copies, waits for them, and re-layouts  9.98 us
    dot_general x27, matrix products, gate_conv(): jnp.einsum('gc,crq->grq', kernel[tap_index], window, preferred_element_ty...  9.61 us
    dot_general x27, matrix products, weight_grads(): jnp.einsum('grq,crq->gc', gate_grad, window, preferred_element_type=jnp.f...  8.87 us
  transfers between devices with their start and end apart: 15, of which 3 were waited for; matrix products, arithmetic and copies ran while one was open for 7% of the time, Pallas kernels for 0%

commit v1 on v0

--- a/solution.py
+++ b/solution.py
@@ -5,6 +5,12 @@
 from jax.sharding import PartitionSpec as P
 
 goal_reach = 64.0
+
+
+def add_all(x, axis):
+    parts = lax.all_gather(x, axis, axis=0, tiled=False)
+    result = parts.sum(axis=0)
+    return result
 
 
 def extended(cells, sides, width):
@@ -141,7 +147,7 @@
             jnp.sum(input_acc * goal_bump, axis=(1, 2)),
         ]
     )
-    grad_table = lax.psum(pieces, ("rows", "maze")) * scale
+    grad_table = add_all(pieces, ("rows", "maze")) * scale
     return (grad_weights, grad_table, carry_hidden[None], carry_cell[None])
 
 

time: 297 us -> 297 us (level)
  blocking collectives: 92.8 us -> 106 us
  waiting for transfers between devices: 84.2 us -> 71.4 us
    all_gather x0 -> x1, blocking collectives: none -> 52.3 us  [add_all(): parts = lax.all_gather(x, axis, axis=0, tiled=False)]
    psum x1 -> x0, blocking collectives: 39.5 us -> none  [per_device(): grad_table = lax.psum(pieces, ('rows', 'maze')) * scale]
    unnamed x2, waiting for transfers between devices: 81.9 us -> 69 us
where the time goes in v1:
time: 297 us; the launch traced here: 296 us
  blocking collectives  106 us (36%)
  waiting for transfers between devices  71.4 us (24%)
  starting transfers between devices  49.7 us (17%)
  matrix products  27.1 us (9%)
  local copies, waits for them, and re-layouts  16 us (5%)
  between operations  15 us (5%)
  other arithmetic  11.1 us (4%)
    unnamed x2, waiting for transfers between devices  69 us
    all_gather x1, blocking collectives, per_device(): lax.all_gather(gate_weights, ('rows', 'maze'), axis=0, tiled=True)  53.3 us
    all_gather x1, blocking collectives, add_all(): parts = lax.all_gather(x, axis, axis=0, tiled=False)  52.3 us
    ppermute x7, starting transfers between devices, extended(): lax.ppermute(head, axis, [((i + 1) % count, i) for i in range(ends)])  36.2 us
    ppermute x7, starting transfers between devices, extended(): lax.ppermute(tail, axis, [(i, (i + 1) % count) for i in range(ends)])  13.4 us
    unnamed x63, local copies, waits for them, and re-layouts  9.98 us
    dot_general x27, matrix products, gate_conv(): jnp.einsum('gc,crq->grq', kernel[tap_index], window, preferred_element_ty...  9.61 us
    dot_general x27, matrix products, weight_grads(): jnp.einsum('grq,crq->gc', gate_grad, window, preferred_element_type=jnp.f...  8.87 us
  transfers between devices with their start and end apart: 15, of which 3 were waited for; matrix products, arithmetic and copies ran while one was open for 7% of the time, Pallas kernels for 0%

profile of v1, /device:TPU:8, one launch (start us, length us, event | category | flops | bytes accessed | tf_op | source)
XLA Modules:
  0.0 295.9 jit_solution(204797417117700422)
XLA Ops:
  7.2 1.3 fusion.286
  9.2 0.8 slice_bitcast_fusion.3
  11.6 1.9 collective-permute-start
  13.5 4.5 %collective-permute-start.1 = (bf16[32,1,256]{2,0,1:T(8,128)(2,1)S(1)}, bf16[32,1,256]{2,0,1:T(8,128)(2,1)S(1)}, u32[]{:S(2)}, u32[]{:S(2)}) collective-permute-start(bf16[32,1,256]{2,0,1:T(8,128)(2,1)S(1)} %get-tuple-element.67), channel_id=1, source_target_pairs={{2,0},{4,2},{6,4},{8,6},{10,8},{12,10},{14,12},{16,14},{18,16},{20... | collective-permute-start | bytes 49160 | tf_op jit(solution)/shard_map/ppermute | solution.py:26
  18.1 0.9 copy.275
  19.0 1.9 collective-permute-start.2
  20.9 4.5 %collective-permute-start.3 = (bf16[32,1,256]{2,0,1:T(8,128)(2,1)S(1)}, bf16[32,1,256]{2,0,1:T(8,128)(2,1)S(1)}, u32[]{:S(2)}, u32[]{:S(2)}) collective-permute-start(bf16[32,1,256]{2,0,1:T(8,128)(2,1)S(1)} %get-tuple-element.69), channel_id=1, source_target_pairs={{2,0},{4,2},{6,4},{8,6},{10,8},{12,10},{14,12},{16,14},{18,16},{20... | collective-permute-start | bytes 49160 | tf_op jit(solution)/shard_map/ppermute | solution.py:26
  26.2 53.3 %all-gather.1 = bf16[32,1,2304]{2,1,0:T(2,128)(2,1)S(1)} all-gather(bf16[1,1,2304]{2,1,0:T(2,128)(2,1)S(1)} %reshape.145), channel_id=1, replica_groups=mesh['rows'=16,'maze'=2] {'rows','maze'}, dimensions={0}, use_global_device_ids=true | all-gather | bytes 152064 | tf_op jit(solution)/shard_map/all_gather | solution.py:71
  79.5 0.8 reduce.1
  85.4 1.9 collective-permute-start.4
  87.4 6.4 %collective-permute-start.5 = (bf16[32,1,256]{2,0,1:T(8,128)(2,1)S(1)}, bf16[32,1,256]{2,0,1:T(8,128)(2,1)S(1)}, u32[]{:S(2)}, u32[]{:S(2)}) collective-permute-start(bf16[32,1,256]{2,0,1:T(8,128)(2,1)S(1)} %get-tuple-element.65), channel_id=1, source_target_pairs={{2,0},{4,2},{6,4},{8,6},{10,8},{12,10},{14,12},{16,14},{18,16},{20... | collective-permute-start | bytes 49160 | tf_op jit(solution)/shard_map/ppermute | solution.py:26
  93.8 1.4 collective-permute-done.5
  98.3 0.9 multiply_convert_fusion.10
  99.2 1.3 fusion.282
  100.6 1.9 collective-permute-start.6
  102.5 4.7 %collective-permute-start.7 = (bf16[32,1,256]{2,0,1:T(8,128)(2,1)}, bf16[32,1,256]{2,0,1:T(8,128)(2,1)}, u32[]{:S(2)}, u32[]{:S(2)}) collective-permute-start(bf16[32,1,256]{2,0,1:T(8,128)(2,1)} %get-tuple-element.63), channel_id=1, source_target_pairs={{2,0},{4,2},{6,4},{8,6},{10,8},{12,10},{14,12},{16,14},{18,16},{20... | collective-permute-start | bytes 49160 | tf_op jit(solution)/shard_map/ppermute | solution.py:26
  108.0 0.9 collective-permute-done.7
  108.8 0.9 maximum_maximum_fusion.2
  109.8 1.1 fusion.180
  116.3 1.9 collective-permute-start.8
  118.3 6.7 %collective-permute-start.9 = (bf16[128,1,256]{2,0,1:T(8,128)(2,1)S(1)}, bf16[128,1,256]{2,0,1:T(8,128)(2,1)S(1)}, u32[]{:S(2)}, u32[]{:S(2)}) collective-permute-start(bf16[128,1,256]{2,0,1:T(8,128)(2,1)S(1)} %get-tuple-element.49), channel_id=1, source_target_pairs={{2,0},{4,2},{6,4},{8,6},{10,8},{12,10},{14,12},{16,14},{18,16},{20... | collective-permute-start | bytes 196616 | tf_op jit(solution)/shard_map/ppermute | solution.py:26
  133.2 1.9 collective-permute-start.10
  135.1 4.6 %collective-permute-start.11 = (bf16[128,1,256]{2,0,1:T(8,128)(2,1)S(1)}, bf16[128,1,256]{2,0,1:T(8,128)(2,1)S(1)}, u32[]{:S(2)}, u32[]{:S(2)}) collective-permute-start(bf16[128,1,256]{2,0,1:T(8,128)(2,1)S(1)} %get-tuple-element.47), channel_id=1, source_target_pairs={{2,0},{4,2},{6,4},{8,6},{10,8},{12,10},{14,12},{16,14},{18,16},{20... | collective-permute-start | bytes 196616 | tf_op jit(solution)/shard_map/ppermute | solution.py:26
  148.1 1.9 collective-permute-start.12
  150.0 4.8 %collective-permute-start.13 = (bf16[128,1,256]{2,0,1:T(8,128)(2,1)S(1)}, bf16[128,1,256]{2,0,1:T(8,128)(2,1)S(1)}, u32[]{:S(2)}, u32[]{:S(2)}) collective-permute-start(bf16[128,1,256]{2,0,1:T(8,128)(2,1)S(1)} %get-tuple-element.45), channel_id=1, source_target_pairs={{2,0},{4,2},{6,4},{8,6},{10,8},{12,10},{14,12},{16,14},{18,16},{20... | collective-permute-start | bytes 196616 | tf_op jit(solution)/shard_map/ppermute | solution.py:26
  157.5 0.9 copy.141
  158.6 0.9 add.360
  163.0 0.7 copy-done.16
  164.8 0.9 copy.140
  165.7 52.3 %all-gather.2 = f32[32,3,32]{2,1,0:T(4,128)S(1)} all-gather(f32[1,3,32]{2,1,0:T(4,128)S(1)} %maximum_bitcast_fusion), channel_id=2, replica_groups=mesh['rows'=16,'maze'=2] {'rows','maze'}, dimensions={0}, use_global_device_ids=true | all-gather | bytes 12672 | tf_op jit(solution)/shard_map/all_gather | solution.py:11
  218.7 69.0 %all-reduce.9.cloned.1.call-done = f32[73728]{0:T(1024)} async-done(((f32[73728]{0:T(1024)}), f32[73728]{0:T(1024)}) %all-reduce.9.cloned.1.call-update) | async-done | bytes 294928
  287.7 1.4 dynamic-slice_multiply_fusion
  (195 shorter events, 41.4 us)
Async XLA Ops:
  7.2 280.5 %all-reduce.9.cloned.1.call-start = ((), (), s32[]{:S(2)}) async-start(), calls=%async_computation | async-start | bytes 589824
  10.7 14.8 %copy-start.25 = (f32[8,256]{1,0:T(8,128)}, f32[8,256]{1,0:T(8,128)S(1)}, u32[]{:S(2)}) copy-start(f32[8,256]{1,0:T(8,128)S(1)} %get-tuple-element.30) | copy-start | bytes 24580
  10.7 14.8 %copy-start.23 = (f32[8,256]{1,0:T(8,128)}, f32[8,256]{1,0:T(8,128)S(1)}, u32[]{:S(2)}) copy-start(f32[8,256]{1,0:T(8,128)S(1)} %convert_bitcast_fusion) | copy-start | bytes 24580
  11.4 14.1 %copy-start.27 = (f32[8,256]{1,0:T(8,128)}, f32[8,256]{1,0:T(8,128)S(1)}, u32[]{:S(2)}) copy-start(f32[8,256]{1,0:T(8,128)S(1)} %multiply_exponential_fusion) | copy-start | bytes 24580
  11.6 69.8 %collective-permute-start = (bf16[32,1,256]{2,0,1:T(8,128)(2,1)S(1)}, bf16[32,1,256]{2,0,1:T(8,128)(2,1)S(1)}, u32[]{:S(2)}, u32[]{:S(2)}) collective-permute-start(bf16[32,1,256]{2,0,1:T(8,128)(2,1)S(1)} %get-tuple-element.66), channel_id=1, source_target_pairs={{0,2},{2,4},{4,6},{6,8},{8,10},{10,12},{12,14},{14,16},{16,18},{18... | collective-permute-start | bytes 49160 | tf_op jit(solution)/shard_map/ppermute | solution.py:24
  13.5 67.9 %collective-permute-start.1 = (bf16[32,1,256]{2,0,1:T(8,128)(2,1)S(1)}, bf16[32,1,256]{2,0,1:T(8,128)(2,1)S(1)}, u32[]{:S(2)}, u32[]{:S(2)}) collective-permute-start(bf16[32,1,256]{2,0,1:T(8,128)(2,1)S(1)} %get-tuple-element.67), channel_id=1, source_target_pairs={{2,0},{4,2},{6,4},{8,6},{10,8},{12,10},{14,12},{16,14},{18,16},{20... | collective-permute-start | bytes 49160 | tf_op jit(solution)/shard_map/ppermute | solution.py:26
  19.0 62.4 %collective-permute-start.2 = (bf16[32,1,256]{2,0,1:T(8,128)(2,1)S(1)}, bf16[32,1,256]{2,0,1:T(8,128)(2,1)S(1)}, u32[]{:S(2)}, u32[]{:S(2)}) collective-permute-start(bf16[32,1,256]{2,0,1:T(8,128)(2,1)S(1)} %get-tuple-element.68), channel_id=1, source_target_pairs={{0,2},{2,4},{4,6},{6,8},{8,10},{10,12},{12,14},{14,16},{16,18},{18... | collective-permute-start | bytes 49160 | tf_op jit(solution)/shard_map/ppermute | solution.py:24
  20.9 60.5 %collective-permute-start.3 = (bf16[32,1,256]{2,0,1:T(8,128)(2,1)S(1)}, bf16[32,1,256]{2,0,1:T(8,128)(2,1)S(1)}, u32[]{:S(2)}, u32[]{:S(2)}) collective-permute-start(bf16[32,1,256]{2,0,1:T(8,128)(2,1)S(1)} %get-tuple-element.69), channel_id=1, source_target_pairs={{2,0},{4,2},{6,4},{8,6},{10,8},{12,10},{14,12},{16,14},{18,16},{20... | collective-permute-start | bytes 49160 | tf_op jit(solution)/shard_map/ppermute | solution.py:26
  80.8 16.8 %copy-start.7 = (bf16[128,64]{1,0:T(8,128)(2,1)}, bf16[128,64]{1,0:T(8,128)(2,1)S(1)}, u32[]{:S(2)}) copy-start(bf16[128,64]{1,0:T(8,128)(2,1)S(1)} %slice.531) | copy-start | bytes 49156
  81.0 15.6 %copy-start.9 = (bf16[128,64]{1,0:T(8,128)(2,1)}, bf16[128,64]{1,0:T(8,128)(2,1)S(1)}, u32[]{:S(2)}) copy-start(bf16[128,64]{1,0:T(8,128)(2,1)S(1)} %slice.522) | copy-start | bytes 49156
  81.2 14.7 %copy-start = (bf16[128,64]{1,0:T(8,128)(2,1)}, bf16[128,64]{1,0:T(8,128)(2,1)S(1)}, u32[]{:S(2)}) copy-start(bf16[128,64]{1,0:T(8,128)(2,1)S(1)} %slice.516) | copy-start | bytes 49156
  81.4 13.8 %copy-start.2 = (bf16[128,64]{1,0:T(8,128)(2,1)}, bf16[128,64]{1,0:T(8,128)(2,1)S(1)}, u32[]{:S(2)}) copy-start(bf16[128,64]{1,0:T(8,128)(2,1)S(1)} %slice.510) | copy-start | bytes 49156
  81.4 13.8 %copy-start.22 = (bf16[32,1,256]{2,0,1:T(8,128)(2,1)}, bf16[32,1,256]{2,0,1:T(8,128)(2,1)S(1)}, u32[]{:S(2)}) copy-start(bf16[32,1,256]{2,0,1:T(8,128)(2,1)S(1)} %collective-permute-done.1) | copy-start | bytes 49156
  84.2 1.0 copy-start.5
  85.4 10.1 %copy-start.12 = (bf16[128,64]{1,0:T(8,128)(2,1)S(1)}, bf16[128,64]{1,0:T(8,128)(2,1)}, u32[]{:S(2)}) copy-start(bf16[128,64]{1,0:T(8,128)(2,1)} %copy-done.11) | copy-start | bytes 49156
  85.4 8.3 %collective-permute-start.4 = (bf16[32,1,256]{2,0,1:T(8,128)(2,1)S(1)}, bf16[32,1,256]{2,0,1:T(8,128)(2,1)S(1)}, u32[]{:S(2)}, u32[]{:S(2)}) collective-permute-start(bf16[32,1,256]{2,0,1:T(8,128)(2,1)S(1)} %get-tuple-element.64), channel_id=1, source_target_pairs={{0,2},{2,4},{4,6},{6,8},{8,10},{10,12},{12,14},{14,16},{16,18},{18... | collective-permute-start | bytes 49160 | tf_op jit(solution)/shard_map/ppermute | solution.py:24
  87.4 7.8 %collective-permute-start.5 = (bf16[32,1,256]{2,0,1:T(8,128)(2,1)S(1)}, bf16[32,1,256]{2,0,1:T(8,128)(2,1)S(1)}, u32[]{:S(2)}, u32[]{:S(2)}) collective-permute-start(bf16[32,1,256]{2,0,1:T(8,128)(2,1)S(1)} %get-tuple-element.65), channel_id=1, source_target_pairs={{2,0},{4,2},{6,4},{8,6},{10,8},{12,10},{14,12},{16,14},{18,16},{20... | collective-permute-start | bytes 49160 | tf_op jit(solution)/shard_map/ppermute | solution.py:26
  98.3 9.0 %copy-start.21 = (bf16[1,3,32,8,256]{4,3,2,1,0:T(8,128)(2,1)S(1)}, bf16[1,3,32,8,256]{4,3,2,1,0:T(8,128)(2,1)}, u32[]{:S(2)}) copy-start(bf16[1,3,32,8,256]{4,3,2,1,0:T(8,128)(2,1)} %param.11) | copy-start | bytes 1179652
  100.6 7.4 %collective-permute-start.6 = (bf16[32,1,256]{2,0,1:T(8,128)(2,1)}, bf16[32,1,256]{2,0,1:T(8,128)(2,1)}, u32[]{:S(2)}, u32[]{:S(2)}) collective-permute-start(bf16[32,1,256]{2,0,1:T(8,128)(2,1)} %get-tuple-element.62), channel_id=1, source_target_pairs={{0,2},{2,4},{4,6},{6,8},{8,10},{10,12},{12,14},{14,16},{16,18},{18... | collective-permute-start | bytes 49160 | tf_op jit(solution)/shard_map/ppermute | solution.py:24
  102.5 6.4 %collective-permute-start.7 = (bf16[32,1,256]{2,0,1:T(8,128)(2,1)}, bf16[32,1,256]{2,0,1:T(8,128)(2,1)}, u32[]{:S(2)}, u32[]{:S(2)}) collective-permute-start(bf16[32,1,256]{2,0,1:T(8,128)(2,1)} %get-tuple-element.63), channel_id=1, source_target_pairs={{2,0},{4,2},{6,4},{8,6},{10,8},{12,10},{14,12},{16,14},{18,16},{20... | collective-permute-start | bytes 49160 | tf_op jit(solution)/shard_map/ppermute | solution.py:26
  108.0 2.9 copy-start.13
  116.3 11.3 %collective-permute-start.8 = (bf16[128,1,256]{2,0,1:T(8,128)(2,1)S(1)}, bf16[128,1,256]{2,0,1:T(8,128)(2,1)S(1)}, u32[]{:S(2)}, u32[]{:S(2)}) collective-permute-start(bf16[128,1,256]{2,0,1:T(8,128)(2,1)S(1)} %get-tuple-element.48), channel_id=1, source_target_pairs={{0,2},{2,4},{4,6},{6,8},{8,10},{10,12},{12,14},{14,16},{16,18},{18... | collective-permute-start | bytes 196616 | tf_op jit(solution)/shard_map/ppermute | solution.py:24
  118.3 9.4 %collective-permute-start.9 = (bf16[128,1,256]{2,0,1:T(8,128)(2,1)S(1)}, bf16[128,1,256]{2,0,1:T(8,128)(2,1)S(1)}, u32[]{:S(2)}, u32[]{:S(2)}) collective-permute-start(bf16[128,1,256]{2,0,1:T(8,128)(2,1)S(1)} %get-tuple-element.49), channel_id=1, source_target_pairs={{2,0},{4,2},{6,4},{8,6},{10,8},{12,10},{14,12},{16,14},{18,16},{20... | collective-permute-start | bytes 196616 | tf_op jit(solution)/shard_map/ppermute | solution.py:26
  131.4 0.9 copy-start.20
  131.6 0.9 copy-start.15
  133.2 9.2 %collective-permute-start.10 = (bf16[128,1,256]{2,0,1:T(8,128)(2,1)S(1)}, bf16[128,1,256]{2,0,1:T(8,128)(2,1)S(1)}, u32[]{:S(2)}, u32[]{:S(2)}) collective-permute-start(bf16[128,1,256]{2,0,1:T(8,128)(2,1)S(1)} %get-tuple-element.46), channel_id=1, source_target_pairs={{0,2},{2,4},{4,6},{6,8},{8,10},{10,12},{12,14},{14,16},{16,18},{18... | collective-permute-start | bytes 196616 | tf_op jit(solution)/shard_map/ppermute | solution.py:24
  135.1 7.3 %collective-permute-start.11 = (bf16[128,1,256]{2,0,1:T(8,128)(2,1)S(1)}, bf16[128,1,256]{2,0,1:T(8,128)(2,1)S(1)}, u32[]{:S(2)}, u32[]{:S(2)}) collective-permute-start(bf16[128,1,256]{2,0,1:T(8,128)(2,1)S(1)} %get-tuple-element.47), channel_id=1, source_target_pairs={{2,0},{4,2},{6,4},{8,6},{10,8},{12,10},{14,12},{16,14},{18,16},{20... | collective-permute-start | bytes 196616 | tf_op jit(solution)/shard_map/ppermute | solution.py:26
  146.5 0.9 copy-start.6
  148.1 11.4 %collective-permute-start.12 = (bf16[128,1,256]{2,0,1:T(8,128)(2,1)S(1)}, bf16[128,1,256]{2,0,1:T(8,128)(2,1)S(1)}, u32[]{:S(2)}, u32[]{:S(2)}) collective-permute-start(bf16[128,1,256]{2,0,1:T(8,128)(2,1)S(1)} %get-tuple-element.44), channel_id=1, source_target_pairs={{0,2},{2,4},{4,6},{6,8},{8,10},{10,12},{12,14},{14,16},{16,18},{18... | collective-permute-start | bytes 196616 | tf_op jit(solution)/shard_map/ppermute | solution.py:24
  150.0 9.5 %collective-permute-start.13 = (bf16[128,1,256]{2,0,1:T(8,128)(2,1)S(1)}, bf16[128,1,256]{2,0,1:T(8,128)(2,1)S(1)}, u32[]{:S(2)}, u32[]{:S(2)}) collective-permute-start(bf16[128,1,256]{2,0,1:T(8,128)(2,1)S(1)} %get-tuple-element.45), channel_id=1, source_target_pairs={{2,0},{4,2},{6,4},{8,6},{10,8},{12,10},{14,12},{16,14},{18,16},{20... | collective-permute-start | bytes 196616 | tf_op jit(solution)/shard_map/ppermute | solution.py:26
  162.7 1.0 copy-start.16
  162.7 1.2 copy-start.18
  (12 other events, 9.4 us)
Sparse Core Ops, SparseCore 0:
  159.6 128.0 all-reduce.8
